TPU v7x, 256 devices: a whole 4x4x8 slice. The times are simulated.
256 devices in a mesh: src: 64 (over z, y_lo, x), rcv: 4 (over y_hi, core).
Axes of the slice: x: 4, y: 4 (y_hi: 2, y_lo: 2; y = y_hi * 2 + y_lo), z: 8, core: 2. Of those that a mesh axis runs over, the one named last changes fastest.
Arguments:
- probes: bfloat16 [256, 1024, 256], P('rcv', 'src'), may hold values from -6 to 6
- kappa: float32 [1024, 256], P('src'), may hold values from 0.02 to 0.24
- footprint: bfloat16 [64, 4, 192, 128, 128], P('src', 'rcv'), may hold values from -0.0390625 to 0.0390625
- block_source: int32 [64, 4, 192], P('src', 'rcv'), may hold values from 0 to 31
- block_receptor: int32 [64, 4, 192], P('src', 'rcv'), may hold values from 0 to 15
- block_count: int32 [64, 4], P('src', 'rcv'), may hold values from 1 to 192, as said below
- obs_weight: float32 [8192], P('rcv'), may hold values from 1 to 8
Outputs:
- hessian_probe: float32 [256, 1024, 256], P('rcv', 'src')
Inputs may be any that keep to these rules, and one draw needn't show every extreme that they name: Slots 0 to block_count - 1 of a tile and group hold its footprint blocks, later slots are unused; some tile and group uses all 192 slots.
All inputs are finite; a program needn't handle non-finite values.
Results may differ from a plain program's by a relative error of at most 0.006.
Values may be sent and summed in bfloat16 or wider, within the bound.
A program may use at most 64 MiB of HBM per device.

v0:
```python
import jax
import jax.numpy as jnp
from jax import lax
from jax.sharding import PartitionSpec as P

BLK = 128
RB_LOC = 16
GROUP = 32
SMOOTH = 4


def extended(shard, sides, width):
    for axis, dim in sides:
        size, length = (lax.axis_size(axis), shard.shape[dim])
        up = [(i, (i + 1) % size) for i in range(size - 1)]
        down = [(j, i) for i, j in up]
        last = lax.slice_in_dim(shard, length - width, length, axis=dim)
        leading = lax.slice_in_dim(shard, 0, width, axis=dim)
        before = lax.ppermute(last, axis, up)
        after = lax.ppermute(leading, axis, down)
        shard = jnp.concatenate([before, shard, after], axis=dim)
    return shard


def laplacian_operator(emission_source_field):
    padded = extended(emission_source_field.astype(jnp.bfloat16), (("src", 1),), 1).astype(
        emission_source_field.dtype
    )
    padded = jnp.pad(padded, ((0, 0), (0, 0), (1, 1)))
    return (
        padded[:, 2:, 1:-1]
        + padded[:, :-2, 1:-1]
        + padded[:, 1:-1, 2:]
        + padded[:, 1:-1, :-2]
        - 4.0 * emission_source_field
    )


def run_groups(step_group, initial, slot_total):
    rounds = slot_total // GROUP
    return lax.fori_loop(
        0, rounds, lambda group_index, running: step_group(group_index * GROUP, running), initial
    )


def per_device(probes, kappa, footprint, block_source, block_receptor, block_count, obs_weight):
    probe_local, lat_rows, lon_cells = probes.shape
    smoothed = probes.astype(jnp.float32)
    for repeat in range(SMOOTH):
        smoothed = smoothed + kappa * laplacian_operator(smoothed)
    local_field = smoothed.astype(jnp.bfloat16)
    gathered = lax.all_gather(local_field, "rcv", axis=0, tiled=True)
    probe_total = gathered.shape[0]
    tile_field = gathered.reshape(probe_total, -1, BLK).transpose(1, 2, 0)
    source_blocks = tile_field.shape[0]
    blocks = footprint.reshape(footprint.shape[2:])
    sources = block_source.reshape(-1)
    receptors = block_receptor.reshape(-1)
    used_slots = block_count.reshape(())
    slot_total = blocks.shape[0]

    def slot_contents(offset):
        block_portion = lax.dynamic_slice_in_dim(blocks, offset, GROUP, 0)
        source_ids = lax.dynamic_slice_in_dim(sources, offset, GROUP, 0)
        receptor_ids = lax.dynamic_slice_in_dim(receptors, offset, GROUP, 0)
        in_use = (offset + jnp.arange(GROUP, dtype=jnp.int32) < used_slots).astype(jnp.float32)
        return (block_portion, source_ids, receptor_ids, in_use)

    def forward_group(offset, running):
        block_portion, source_ids, receptor_ids, in_use = slot_contents(offset)
        selected_entries = jnp.take(tile_field, source_ids, axis=0)
        hessian_result = jnp.einsum(
            "wlq,wqd->wld", block_portion, selected_entries, preferred_element_type=jnp.float32
        )
        return running.at[receptor_ids].add(hessian_result * in_use[:, None, None])

    evolved = run_groups(
        forward_group, jnp.zeros((RB_LOC, BLK, probe_total), jnp.float32), slot_total
    )
    sim_rows = evolved.reshape(-1, probe_total)
    receptor_all = lax.psum(sim_rows, "src")
    weighted = (obs_weight[:, None] * receptor_all).astype(jnp.bfloat16)
    weighted = weighted.reshape(RB_LOC, BLK, probe_total)

    def adjoint_group(offset, running):
        block_portion, source_ids, receptor_ids, in_use = slot_contents(offset)
        selected_entries = jnp.take(weighted, receptor_ids, axis=0)
        hessian_result = jnp.einsum(
            "grc,grp->pgc", block_portion, selected_entries, preferred_element_type=jnp.float32
        )
        return running.at[:, source_ids].add(hessian_result * in_use[None, :, None])

    adjoint_terms = run_groups(
        adjoint_group, jnp.zeros((probe_total, source_blocks, BLK), jnp.float32), slot_total
    )
    adjoint_rows = adjoint_terms.reshape(probe_total, lat_rows, lon_cells).astype(jnp.bfloat16)
    back = lax.psum_scatter(adjoint_rows, "rcv", scatter_dimension=0, tiled=True).astype(
        jnp.float32
    )
    for repeat in range(SMOOTH):
        back = back + laplacian_operator(kappa * back)
    return probes.astype(jnp.float32) + back


def solution(mesh):
    placed = (
        P("rcv", "src", None),
        P("src", None),
        P("src", "rcv", None, None, None),
        P("src", "rcv", None),
        P("src", "rcv", None),
        P("src", "rcv"),
        P("rcv"),
    )
    return jax.shard_map(
        per_device, mesh=mesh, in_specs=placed, out_specs=P("rcv", "src", None), check_vma=False
    )
```

profile of v0, /device:TPU:1, one launch (start us, length us, event | category | flops | bytes accessed | tf_op | source)
XLA Modules:
  0.0 1005.0 jit_solution(7618383937822140229)
XLA Ops:
  7.7 3.9 collective-permute-start
  13.0 3.7 collective-permute-done.1
  23.5 3.7 collective-permute-done.3
  28.4 4.7 collective-permute-start.4
  34.4 3.7 collective-permute-done.5
  39.3 4.0 collective-permute-start.6
  44.7 4.0 collective-permute-done.7
  50.6 46.8 %all-gather.2.cloned.1.call-done = bf16[256,16,256]{2,1,0:T(8,128)(2,1)} async-done(((bf16[64,16,256]{2,1,0:T(8,128)(2,1)}), bf16[256,16,256]{2,1,0:T(8,128)(2,1)}) %all-gather.2.cloned.1.call-update) | async-done | bytes 2097168 | tf_op jit(solution)/shard_map/all_gather | solution.py:52
  97.4 4.3 copy.15
  102.4 94.1 %while.26 = (s32[]{:T(128)}, f32[16,128,256]{2,1,0:T(8,128)S(1)}, s32[192]{0:T(256)S(1)}, bf16[192,128,128]{2,1,0:T(8,128)(2,1)}, s32[192]{0:T(256)S(1)}, /*inde...) while((s32[]{:T(128)}, f32[16,128,256]{2,1,0:T(8,128)S(1)}, ...), condition=%wide.region_2.3_spmd, body=%wide.region_0.2_spmd.sunk | while | flops 271582592 | bytes 24122736 | solution.py:41
  103.2 3.7 gather_fusion
  106.9 4.7 convolution_multiply_fusion.4
  111.6 6.5 scatter_fusion
  118.9 3.7 gather_fusion
  122.6 4.7 convolution_multiply_fusion.4
  127.3 6.5 scatter_fusion
  134.6 3.7 gather_fusion
  138.3 4.7 convolution_multiply_fusion.4
  143.0 6.5 scatter_fusion
  150.3 3.7 gather_fusion
  154.0 4.7 convolution_multiply_fusion.4
  158.7 6.5 scatter_fusion
  166.0 3.7 gather_fusion
  169.7 4.7 convolution_multiply_fusion.4
  174.3 6.5 scatter_fusion
  185.3 4.7 convolution_multiply_fusion.4
  190.0 6.5 scatter_fusion
  198.1 570.0 %all-reduce.10.cloned.1.call-done = f32[2048,256]{1,0:T(8,128)} async-done(((f32[2048,256]{1,0:T(8,128)}), f32[2048,256]{1,0:T(8,128)}) %all-reduce.10.cloned.1.call-update) | async-done | bytes 2097168 | tf_op jit(solution)/shard_map/psum | solution.py:81
  772.6 93.6 %while.27 = (s32[]{:T(128)}, f32[256,32,128]{2,0,1:T(8,128)}, s32[192]{0:T(256)S(1)}, s32[192]{0:T(256)S(1)}, bf16[16,128,256]{2,1,0:T(8,128)(2,1)S(1)}, /*index...) while((s32[]{:T(128)}, f32[256,32,128]{2,0,1:T(8,128)}, ...), condition=%wide.region_6.7_spmd, body=%wide.region_4.6_spmd.sunk | while | flops 271582592 | bytes 24122736 | solution.py:41
  774.1 4.2 convolution_multiply_fusion.5
  778.3 9.8 scatter_fusion.1
  789.7 4.2 convolution_multiply_fusion.5
  793.9 9.9 scatter_fusion.1
  805.3 4.2 convolution_multiply_fusion.5
  809.6 9.9 scatter_fusion.1
  821.0 4.2 convolution_multiply_fusion.5
  825.2 9.8 scatter_fusion.1
  836.5 4.2 convolution_multiply_fusion.5
  840.8 9.8 scatter_fusion.1
  852.1 4.2 convolution_multiply_fusion.5
  856.3 9.8 scatter_fusion.1
  872.2 84.6 %reduce-scatter.2.cloned.1.call-done = bf16[64,16,256]{2,1,0:T(8,128)(2,1)} async-done(((bf16[256,16,256]{2,1,0:T(8,128)(2,1)}), bf16[64,16,256]{2,1,0:T(8,128)(2,1)}) %reduce-scatter.2.cloned.1.call-update) | async-done | bytes 524304 | tf_op jit(solution)/shard_map/reduce_scatter | solution.py:97
  962.6 3.7 collective-permute-done.9
  971.9 3.7 collective-permute-done.11
  976.9 3.8 collective-permute-start.12
  981.9 3.7 collective-permute-done.13
  986.9 4.3 collective-permute-start.14
  992.5 3.9 collective-permute-done.15
  (115 shorter events, 64.9 us)
Async XLA Ops:
  6.5 11.6 %copy-start.1 = (bf16[64,16,256]{2,1,0:T(8,128)(2,1)S(1)}, bf16[64,16,256]{2,1,0:T(8,128)(2,1)}, u32[]{:S(2)}) copy-start(bf16[64,16,256]{2,1,0:T(8,128)(2,1)} %param.11) | copy-start | bytes 1572868
  6.5 11.6 %copy-start.4 = (f32[16,256]{1,0:T(8,128)S(1)}, f32[16,256]{1,0:T(8,128)}, u32[]{:S(2)}) copy-start(f32[16,256]{1,0:T(8,128)} %param.12) | copy-start | bytes 49156
  6.5 90.9 %all-gather.2.cloned.1.call-start = ((), (), s32[]{:S(2)}) async-start(), calls=%async_computation.1 | async-start | bytes 2621440 | tf_op jit(solution)/shard_map/all_gather | solution.py:52
  7.7 5.3 collective-permute-start
  11.7 5.0 collective-permute-start.1
  19.0 4.4 collective-permute-start.2
  22.1 5.0 collective-permute-start.3
  28.4 6.0 collective-permute-start.4
  33.1 5.0 collective-permute-start.5
  39.3 5.3 collective-permute-start.6
  43.3 5.3 collective-permute-start.7
  50.6 717.6 %all-reduce.10.cloned.1.call-start = ((), (), s32[]{:S(2)}) async-start(), calls=%async_computation.2 | async-start | bytes 4194304 | tf_op jit(solution)/shard_map/psum | solution.py:81
  101.7 0.7 copy-start.6
  101.7 0.7 copy-start.7
  196.5 1.3 copy-start
  196.5 571.6 %copy-start.5 = (f32[2048]{0:T(1024)S(1)}, f32[2048]{0:T(1024)}, u32[]{:S(2)}) copy-start(f32[2048]{0:T(1024)} %param.17) | copy-start | bytes 24580
  197.9 759.0 %reduce-scatter.2.cloned.1.call-start = ((), (), s32[]{:S(2)}) async-start(), calls=%async_computation.3 | async-start | bytes 2621440 | tf_op jit(solution)/shard_map/reduce_scatter | solution.py:97
  956.8 9.9 copy-start.3
  958.2 4.4 collective-permute-start.8
  961.3 5.0 collective-permute-start.9
  967.5 4.4 collective-permute-start.10
  970.6 5.0 collective-permute-start.11
  976.9 5.1 collective-permute-start.12
  980.6 5.0 collective-permute-start.13
  986.7 10.0 copy-start.2
  986.9 5.6 collective-permute-start.14
  991.2 5.2 collective-permute-start.15
Sparse Core Ops, SparseCore 0:
  50.7 46.6 all-gather.1
  198.0 570.0 all-reduce.9
  872.4 84.4 reduce-scatter.1
where the time goes:
time: 1020 us; the launch traced here: 1000 us
  waiting for transfers between devices  732 us (72%)
  other arithmetic  125 us (12%)
  matrix products  53.5 us (5%)
  starting transfers between devices  40.6 us (4%)
  local copies, waits for them, and re-layouts  40.5 us (4%)
  between operations  13.5 us (1%)
    psum x1, waiting for transfers between devices, per_device(): receptor_all = lax.psum(sim_rows, 'src')  570 us
    reduce_scatter x1, waiting for transfers between devices, per_device(): lax.psum_scatter(adjoint_rows, 'rcv', scatter_dimension=0, tiled=True)  84.6 us
    scatter-add x6, other arithmetic, adjoint_group(): return running.at[:, source_ids].add(hessian_result * in_use[None, :, None])  59.1 us
    all_gather x1, waiting for transfers between devices, per_device(): gathered = lax.all_gather(local_field, 'rcv', axis=0, tiled=True)  46.8 us
    scatter-add x6, other arithmetic, forward_group(): return running.at[receptor_ids].add(hessian_result * in_use[:, None, None])  38.9 us
    ppermute x8, starting transfers between devices, extended(): before = lax.ppermute(last, axis, up)  30 us
    ppermute x8, waiting for transfers between devices, extended(): after = lax.ppermute(leading, axis, down)  30 us
    dot_general x6, matrix products, forward_group(): jnp.einsum('wlq,wqd->wld', block_portion, selected_entries, preferred_ele...  28.1 us
  transfers between devices with their start and end apart: 19, of which 11 were waited for; matrix products, arithmetic and copies ran while one was open for 0% of the time, Pallas kernels for 0%

commit v1 on v0

v1 whole, which is shorter than its diff:
```python
import jax
import jax.numpy as jnp
from jax import lax
from jax.experimental import pallas as pl
from jax.experimental.pallas import tpu as pltpu
from jax.sharding import PartitionSpec as P

BLK = 128
RB = 16
SB = 32
NB = 192
LAT = 16
LON = 256
PROBES = 64
GROUPS = 4
GP = PROBES // GROUPS
STEPS = 4
PAD = LAT + 2 * STEPS
CHUNK = 16
NCHUNK = NB // CHUNK
N_SRC = 64
MESH = pl.DeviceIdType.MESH
F32 = jnp.float32
BF16 = jnp.bfloat16
VM = pl.BlockSpec(memory_space=pltpu.VMEM)
SM = pl.BlockSpec(memory_space=pltpu.SMEM)
ANY = pl.BlockSpec(memory_space=pl.ANY)
DMA = pltpu.SemaphoreType.DMA


def remote(src, dst, send, recv, device):
    return pltpu.make_async_remote_copy(
        src_ref=src, dst_ref=dst, send_sem=send, recv_sem=recv, device_id=device, device_id_type=MESH
    )


def meet(peers):
    barrier = pltpu.get_barrier_semaphore()
    for peer in peers:
        pl.semaphore_signal(barrier, inc=1, device_id=peer, device_id_type=MESH)
    pl.semaphore_wait(barrier, len(peers))


def ring_places():
    s = lax.axis_index("src")
    r = lax.axis_index("rcv")
    y_lo = lax.rem(s // 4, 2)
    pair = s + 4 - 8 * y_lo
    y_hi = r // 2
    core = lax.rem(r, 2)
    other = lax.rem(r + 2, 4)
    sib_r = y_hi * 2 + 1 - core
    far_sib_r = (1 - y_hi) * 2 + 1 - core
    plus = (pair, lax.rem(r + 2 * y_lo, 4))
    minus = (pair, lax.rem(r + 2 * (1 - y_lo), 4))
    north = (lax.rem(s + N_SRC - 1, N_SRC), r)
    south = (lax.rem(s + 1, N_SRC), r)
    return s, r, other, sib_r, far_sib_r, plus, minus, north, south


def onward(group, plus, minus):
    even = lax.rem(group, 2) == 0
    return (plus[0], jnp.where(even, plus[1], minus[1]))


def west_east(value, lane):
    west = jnp.where(lane == 0, 0.0, pltpu.roll(value, 1, 1))
    east = jnp.where(lane == LON - 1, 0.0, pltpu.roll(value, LON - 1, 1))
    return west + east


def smooth_gather(
    probes_ref, kappa_ref, out_ref, kext_ref,
    xl, xr, xt, kb, fa, fb, relay,
    halo_send, halo_recv, sib_send, sib_recv, out_send, out_recv, rel_send, rel_recv, fwd_send, fwd_recv,
):
    s, r, other, sib_r, far_sib_r, plus, minus, north, south = ring_places()
    sib = (s, sib_r)
    xl[...] = probes_ref[:, :BLK].astype(F32)
    xr[...] = probes_ref[:, BLK:].astype(F32)
    for l in list(range(STEPS)) + list(range(LAT - STEPS, LAT)) + list(range(STEPS, LAT - STEPS)):
        rows = pl.ds(l, PROBES, stride=LAT)
        xt[STEPS + l, :, :BLK] = xl[rows, :].astype(BF16)
        xt[STEPS + l, :, BLK:] = xr[rows, :].astype(BF16)
    kext_ref[pl.ds(8, LAT), :] = kappa_ref[...]
    meet((north, south, sib, plus, minus))
    halos = [
        remote(xt.at[pl.ds(STEPS, STEPS)], xt.at[pl.ds(STEPS + LAT, STEPS)], halo_send.at[0], halo_recv.at[0], north),
        remote(xt.at[pl.ds(LAT, STEPS)], xt.at[pl.ds(0, STEPS)], halo_send.at[1], halo_recv.at[1], south),
        remote(kappa_ref.at[pl.ds(0, 8)], kext_ref.at[pl.ds(24, 8)], halo_send.at[2], halo_recv.at[2], north),
        remote(kappa_ref.at[pl.ds(8, 8)], kext_ref.at[pl.ds(0, 8)], halo_send.at[3], halo_recv.at[3], south),
    ]
    for copy in halos:
        copy.start()
    for copy in halos:
        copy.wait()
    north_in = jnp.where(s > 0, 1.0, 0.0).astype(F32)
    south_in = jnp.where(s < N_SRC - 1, 1.0, 0.0).astype(F32)
    kext_ref[pl.ds(0, 8), :] = kext_ref[pl.ds(0, 8), :] * north_in
    kext_ref[pl.ds(24, 8), :] = kext_ref[pl.ds(24, 8), :] * south_in
    for l in range(PAD):
        kb[l] = jnp.broadcast_to(kext_ref[pl.ds(l + 4, 1), :], (GP, LON))
    lane = lax.broadcasted_iota(jnp.int32, (GP, LON), 1)

    def sibling_copy(g):
        return remote(out_ref.at[r, :, g], out_ref.at[r, :, g], sib_send.at[g], sib_recv.at[g], sib)

    def outward_copy(g):
        return remote(out_ref.at[r, :, g], relay.at[g], out_send.at[g], out_recv.at[g], onward(g, plus, minus))

    def relay_copy(g):
        even = lax.rem(g, 2) == 0
        slot = jnp.where(even, minus[1], plus[1])
        return remote(relay.at[g], out_ref.at[slot, :, g], rel_send.at[g], rel_recv.at[g], onward(g, plus, minus))

    def share_copy(g):
        return remote(out_ref.at[other, :, g], out_ref.at[other, :, g], fwd_send.at[g], fwd_recv.at[g], sib)

    def one_group(g, carry):
        rows = pl.ds(pl.multiple_of(g * GP, GP), GP)
        for l in range(PAD):
            scale = north_in if l < STEPS else south_in if l >= STEPS + LAT else None
            value = xt[l, rows, :].astype(F32)
            fa[l] = value if scale is None else value * scale
        for step in range(STEPS):
            old, new = (fa, fb) if step % 2 == 0 else (fb, fa)
            for l in range(step + 1, PAD - step - 1):
                c = old[l]
                v = c + kb[l] * (old[l - 1] + old[l + 1] + west_east(c, lane) - 4.0 * c)
                if step < STEPS - 1:
                    new[l] = v
                else:
                    j = 2 * (l - STEPS)
                    out_ref[r, j, g] = v[:, :BLK].astype(BF16)
                    out_ref[r, j + 1, g] = v[:, BLK:].astype(BF16)
        outward_copy(g).start()
        sibling_copy(g).start()
        return carry

    lax.fori_loop(0, GROUPS, one_group, 0)

    def pass_on(g, carry):
        outward_copy(g).wait_recv()
        relay_copy(g).start()
        return carry

    lax.fori_loop(0, GROUPS, pass_on, 0)

    def share(g, carry):
        relay_copy(g).wait_recv()
        share_copy(g).start()
        return carry

    lax.fori_loop(0, GROUPS, share, 0)

    def drain(g, carry):
        outward_copy(g).wait_send()
        sibling_copy(g).wait()
        relay_copy(g).wait_send()
        share_copy(g).wait()
        return carry

    lax.fori_loop(0, GROUPS, drain, 0)


def forward_blocks(src_ref, rec_ref, cnt_ref, field_ref, blocks_hbm, out_ref, acc, blocks, sems):
    copies = [
        pltpu.make_async_copy(blocks_hbm.at[pl.ds(c * CHUNK, CHUNK)], blocks.at[pl.ds(c * CHUNK, CHUNK)], sems.at[c])
        for c in range(NCHUNK)
    ]
    for copy in copies:
        copy.start()
    count = cnt_ref[0]

    def clear(b, carry):
        acc[b] = jnp.zeros((4 * PROBES, BLK), F32)
        return carry

    lax.fori_loop(0, RB + 1, clear, 0)

    def four(q, carry):
        terms = []
        for u in range(4):
            n = q * 4 + u
            lhs = field_ref[:, src_ref[n]].reshape(4 * PROBES, BLK)
            terms.append(
                lax.dot_general(lhs, blocks[n], (((1,), (1,)), ((), ())), preferred_element_type=F32)
            )
        for u in range(4):
            n = q * 4 + u
            b = jnp.where(n < count, rec_ref[n], RB)
            acc[b] = acc[b] + terms[u]
        return carry

    for c in range(NCHUNK):
        copies[c].wait()
        quads = jnp.clip((count - c * CHUNK + 3) // 4, 0, CHUNK // 4)
        lax.fori_loop(c * (CHUNK // 4), c * (CHUNK // 4) + quads, four, 0)

    def finish(b, carry):
        for q in range(4):
            out_ref[q, b] = acc[b, q * PROBES : (q + 1) * PROBES, :].astype(BF16)
        return carry

    lax.fori_loop(0, RB, finish, 0)


def adjoint_blocks(src_ref, rec_ref, cnt_ref, weighted_ref, blocks_hbm, out_ref, acc, blocks, sems):
    copies = [
        pltpu.make_async_copy(blocks_hbm.at[pl.ds(c * CHUNK, CHUNK)], blocks.at[pl.ds(c * CHUNK, CHUNK)], sems.at[c])
        for c in range(NCHUNK)
    ]
    for copy in copies:
        copy.start()
    count = cnt_ref[0]

    def clear(b, carry):
        acc[b] = jnp.zeros((4 * PROBES, BLK), F32)
        return carry

    lax.fori_loop(0, SB + 1, clear, 0)

    def four(q, carry):
        terms = []
        for u in range(4):
            n = q * 4 + u
            lhs = weighted_ref[:, rec_ref[n]].reshape(4 * PROBES, BLK)
            terms.append(
                lax.dot_general(lhs, blocks[n], (((1,), (0,)), ((), ())), preferred_element_type=F32)
            )
        for u in range(4):
            n = q * 4 + u
            b = jnp.where(n < count, src_ref[n], SB)
            acc[b] = acc[b] + terms[u]
        return carry

    for c in range(NCHUNK):
        copies[c].wait()
        quads = jnp.clip((count - c * CHUNK + 3) // 4, 0, CHUNK // 4)
        lax.fori_loop(c * (CHUNK // 4), c * (CHUNK // 4) + quads, four, 0)

    def finish(b, carry):
        for q in range(4):
            out_ref[q, b] = acc[b, q * PROBES : (q + 1) * PROBES, :].astype(BF16)
        return carry

    lax.fori_loop(0, SB, finish, 0)


HALF = RB // 2


def reduce_weight_gather(
    part_ref, weight_ref, out_ref,
    a_east, a_west, s_east, s_west, d_lo, d_hi, b_lo, b_hi, total, landed,
    x_send, x_recv, z_send, z_recv, a_send, a_recv, g_send, g_recv,
):
    s = lax.axis_index("src")
    r = lax.axis_index("rcv")
    x = lax.rem(s, 4)
    b0 = s // 4
    xe = lax.rem(x + 1, 4)
    xw = lax.rem(x + 3, 4)
    xo = lax.rem(x + 2, 4)
    east = (b0 * 4 + xe, r)
    west = (b0 * 4 + xw, r)

    def peer(k):
        return (lax.rem(b0 + k, RB) * 4 + x, r)

    barrier = pltpu.get_barrier_semaphore()
    pl.semaphore_signal(barrier, inc=1, device_id=east, device_id_type=MESH)
    pl.semaphore_signal(barrier, inc=1, device_id=west, device_id_type=MESH)

    def greet(k, carry):
        pl.semaphore_signal(barrier, inc=1, device_id=peer(k), device_id_type=MESH)
        return carry

    lax.fori_loop(1, RB, greet, 0)
    pl.semaphore_wait(barrier, RB + 1)

    lo, hi = pl.ds(0, HALF), pl.ds(HALF, HALF)
    first_east = remote(part_ref.at[xo, lo], a_east, x_send.at[0], x_recv.at[0], east)
    first_west = remote(part_ref.at[xo, hi], a_west, x_send.at[1], x_recv.at[1], west)
    direct_east = remote(part_ref.at[xe, hi], d_hi, x_send.at[2], x_recv.at[2], east)
    direct_west = remote(part_ref.at[xw, lo], d_lo, x_send.at[3], x_recv.at[3], west)
    second_east = remote(s_east, b_lo, x_send.at[4], x_recv.at[4], east)
    second_west = remote(s_west, b_hi, x_send.at[5], x_recv.at[5], west)
    for copy in (first_east, first_west, direct_east, direct_west):
        copy.start()
    first_east.wait_recv()
    for b in range(HALF):
        s_east[b] = (a_east[b].astype(F32) + part_ref[xe, b].astype(F32)).astype(BF16)
    second_east.start()
    first_west.wait_recv()
    for b in range(HALF):
        s_west[b] = (a_west[b].astype(F32) + part_ref[xw, HALF + b].astype(F32)).astype(BF16)
    second_west.start()
    direct_east.wait_recv()
    direct_west.wait_recv()
    second_east.wait_recv()
    for b in range(HALF):
        total[b] = (part_ref[x, b].astype(F32) + d_lo[b].astype(F32) + b_lo[b].astype(F32)).astype(BF16)
    second_west.wait_recv()
    for b in range(HALF):
        total[HALF + b] = (
            part_ref[x, HALF + b].astype(F32) + d_hi[b].astype(F32) + b_hi[b].astype(F32)
        ).astype(BF16)

    def scatter_copy(k):
        return remote(total.at[lax.rem(b0 + k, RB)], landed.at[k], z_send.at[k], z_recv.at[k], peer(k))

    def scatter(k, carry):
        scatter_copy(k).start()
        return carry

    lax.fori_loop(1, RB, scatter, 0)

    def collect(k, running):
        scatter_copy(k).wait_recv()
        return running + landed[k].astype(F32)

    evolved = lax.fori_loop(1, RB, collect, total[b0].astype(F32))
    out_ref[x, b0] = (evolved * weight_ref[pl.ds(b0, 1), :]).astype(BF16)

    def gather_copy(k):
        return remote(out_ref.at[x, b0], out_ref.at[x, b0], a_send.at[k], a_recv.at[k], peer(k))

    def gather(k, carry):
        gather_copy(k).start()
        return carry

    def gathered(k, carry):
        slot = lax.rem(b0 + RB - k, RB)
        remote(out_ref.at[x, slot], out_ref.at[x, slot], a_send.at[k], a_recv.at[k], peer(k)).wait_recv()
        return carry

    lax.fori_loop(1, RB, gather, 0)
    lax.fori_loop(1, RB, gathered, 0)

    def along(q, part, n, device):
        return remote(out_ref.at[q, part], out_ref.at[q, part], g_send.at[n], g_recv.at[n], device)

    for copy in (along(x, lo, 0, east), along(x, hi, 1, west), along(x, hi, 2, east), along(x, lo, 3, west)):
        copy.start()
    along(xw, lo, 0, east).wait_recv()
    along(xw, lo, 4, east).start()
    along(xe, hi, 1, west).wait_recv()
    along(xe, hi, 5, west).start()
    along(xw, hi, 2, east).wait_recv()
    along(xe, lo, 3, west).wait_recv()
    along(xo, lo, 4, east).wait_recv()
    along(xo, hi, 5, west).wait_recv()

    def drain(k, carry):
        scatter_copy(k).wait_send()
        gather_copy(k).wait_send()
        return carry

    lax.fori_loop(1, RB, drain, 0)
    for copy in (first_east, first_west, direct_east, direct_west, second_east, second_west):
        copy.wait_send()
    along(x, lo, 0, east).wait_send()
    along(x, hi, 1, west).wait_send()
    along(x, hi, 2, east).wait_send()
    along(x, lo, 3, west).wait_send()
    along(xw, lo, 4, east).wait_send()
    along(xe, hi, 5, west).wait_send()


def combine_smooth(
    part_ref, kext_ref, probes_ref, out_ref,
    xl, xr, kb, fa, fb, adj, sib_far, sib_own, pre, relay, far, edge_out, edge_in,
    sf_send, sf_recv, so_send, so_recv, out_send, out_recv, rel_send, rel_recv, n_send, n_recv, s_send, s_recv,
):
    s, r, other, sib_r, far_sib_r, plus, minus, north, south = ring_places()
    sib = (s, sib_r)
    meet((north, south, sib, plus, minus))

    def sib_far_copy(g):
        return remote(part_ref.at[far_sib_r, :, g], sib_far.at[g], sf_send.at[g], sf_recv.at[g], sib)

    def sib_own_copy(g):
        return remote(part_ref.at[sib_r, :, g], sib_own.at[g], so_send.at[g], so_recv.at[g], sib)

    def outward_copy(g):
        return remote(pre.at[g], relay.at[g], out_send.at[g], out_recv.at[g], onward(g, plus, minus))

    def relay_copy(g):
        return remote(relay.at[g], far.at[g], rel_send.at[g], rel_recv.at[g], onward(g, plus, minus))

    def north_copy(g):
        return remote(edge_out.at[g, 0], edge_in.at[g, 1], n_send.at[g], n_recv.at[g], north)

    def south_copy(g):
        return remote(edge_out.at[g, 1], edge_in.at[g, 0], s_send.at[g], s_recv.at[g], south)

    def begin(g, carry):
        sib_far_copy(g).start()
        return carry

    lax.fori_loop(0, GROUPS, begin, 0)

    def begin_own(g, carry):
        sib_own_copy(g).start()
        return carry

    lax.fori_loop(0, GROUPS, begin_own, 0)

    def presum(g, carry):
        sib_far_copy(g).wait_recv()

        def block(j, inner):
            pre[g, j] = (part_ref[other, j, g].astype(F32) + sib_far[g, j].astype(F32)).astype(BF16)
            return inner

        lax.fori_loop(0, SB, block, 0, unroll=8)
        outward_copy(g).start()
        return carry

    lax.fori_loop(0, GROUPS, presum, 0)
    xl[...] = probes_ref[:, :BLK].astype(F32)
    xr[...] = probes_ref[:, BLK:].astype(F32)
    for l in range(PAD):
        kb[l] = jnp.broadcast_to(kext_ref[pl.ds(l + 4, 1), :], (GP, LON))
    lane = lax.broadcasted_iota(jnp.int32, (GP, LON), 1)

    def pass_on(g, carry):
        outward_copy(g).wait_recv()
        relay_copy(g).start()
        return carry

    lax.fori_loop(0, GROUPS, pass_on, 0)

    def finish_sum(g):
        sib_own_copy(g).wait_recv()
        relay_copy(g).wait_recv()
        for l in range(LAT):
            for h in range(2):
                j = 2 * l + h
                value = part_ref[r, j, g].astype(F32) + sib_own[g, j].astype(F32) + far[g, j].astype(F32)
                adj[g, l, :, h * BLK : (h + 1) * BLK] = value
                if l < STEPS:
                    edge_out[g, 0, l, :, h * BLK : (h + 1) * BLK] = value.astype(BF16)
                if l >= LAT - STEPS:
                    edge_out[g, 1, l - LAT + STEPS, :, h * BLK : (h + 1) * BLK] = value.astype(BF16)
        north_copy(g).start()
        south_copy(g).start()

    def smooth(g):
        north_copy(g).wait_recv()
        south_copy(g).wait_recv()
        for l in range(STEPS):
            fa[l] = edge_in[g, 0, l].astype(F32)
            fa[STEPS + LAT + l] = edge_in[g, 1, l].astype(F32)
        for l in range(LAT):
            fa[STEPS + l] = adj[g, l]
        base = pl.multiple_of(g * (GP * LAT), GP * LAT)
        for step in range(STEPS):
            for l in range(step, PAD - step):
                fb[l] = kb[l] * fa[l]
            for l in range(step + 1, PAD - step - 1):
                c = fb[l]
                v = fa[l] + (fb[l - 1] + fb[l + 1] + west_east(c, lane) - 4.0 * c)
                if step < STEPS - 1:
                    fa[l] = v
                else:
                    rows = pl.ds(base + l - STEPS, GP, stride=LAT)
                    xl[rows, :] = xl[rows, :] + v[:, :BLK]
                    xr[rows, :] = xr[rows, :] + v[:, BLK:]
        done = pl.ds(base, GP * LAT)
        out_ref[done, :BLK] = xl[done, :]
        out_ref[done, BLK:] = xr[done, :]

    def stage(g, carry):
        @pl.when(g < GROUPS)
        def _():
            finish_sum(g)

        @pl.when(g > 0)
        def _():
            smooth(g - 1)

        return carry

    lax.fori_loop(0, GROUPS + 1, stage, 0)

    def drain(g, carry):
        sib_far_copy(g).wait_send()
        sib_own_copy(g).wait_send()
        outward_copy(g).wait_send()
        relay_copy(g).wait_send()
        north_copy(g).wait_send()
        south_copy(g).wait_send()
        return carry

    lax.fori_loop(0, GROUPS, drain, 0)


def remote_params(n):
    return pltpu.CompilerParams(collective_id=n, has_side_effects=True)


def per_device(probes, kappa, footprint, block_source, block_receptor, block_count, obs_weight):
    flat = probes.reshape(PROBES * LAT, LON)
    blocks = footprint.reshape(NB, BLK, BLK)
    sources = block_source.reshape(NB)
    receptors = block_receptor.reshape(NB)
    count = block_count.reshape(1)
    pieces = (4, SB, GROUPS, GP, BLK)
    gathered, kext = pl.pallas_call(
        smooth_gather,
        out_shape=(jax.ShapeDtypeStruct(pieces, BF16), jax.ShapeDtypeStruct((32, LON), F32)),
        in_specs=[VM, VM],
        out_specs=(VM, VM),
        scratch_shapes=[
            pltpu.VMEM((PROBES * LAT, BLK), F32),
            pltpu.VMEM((PROBES * LAT, BLK), F32),
            pltpu.VMEM((PAD, PROBES, LON), BF16),
            pltpu.VMEM((PAD, GP, LON), F32),
            pltpu.VMEM((PAD, GP, LON), F32),
            pltpu.VMEM((PAD, GP, LON), F32),
            pltpu.VMEM((GROUPS, SB, GP, BLK), BF16),
        ]
        + [DMA((4,))] * 10,
        compiler_params=remote_params(0),
        name="smooth_gather",
    )(flat, kappa)
    part = pl.pallas_call(
        forward_blocks,
        out_shape=jax.ShapeDtypeStruct((4, RB, PROBES, BLK), BF16),
        in_specs=[SM, SM, SM, VM, ANY],
        out_specs=VM,
        scratch_shapes=[
            pltpu.VMEM((RB + 1, 4 * PROBES, BLK), F32),
            pltpu.VMEM((NB, BLK, BLK), BF16),
            DMA((NCHUNK,)),
        ],
        name="forward_blocks",
    )(sources, receptors, count, gathered.reshape(4, SB, PROBES, BLK), blocks)
    half = pltpu.VMEM((HALF, PROBES, BLK), BF16)
    whole = pltpu.VMEM((RB, PROBES, BLK), BF16)
    weighted = pl.pallas_call(
        reduce_weight_gather,
        out_shape=jax.ShapeDtypeStruct((4, RB, PROBES, BLK), BF16),
        in_specs=[VM, VM],
        out_specs=VM,
        scratch_shapes=[half] * 8
        + [whole] * 2
        + [DMA((6,)), DMA((6,)), DMA((RB,)), DMA((RB,)), DMA((RB,)), DMA((RB,)), DMA((6,)), DMA((6,))],
        compiler_params=remote_params(1),
        name="reduce_weight_gather",
    )(part, obs_weight.reshape(RB, BLK))
    terms = pl.pallas_call(
        adjoint_blocks,
        out_shape=jax.ShapeDtypeStruct((4, SB, PROBES, BLK), BF16),
        in_specs=[SM, SM, SM, VM, ANY],
        out_specs=VM,
        scratch_shapes=[
            pltpu.VMEM((SB + 1, 4 * PROBES, BLK), F32),
            pltpu.VMEM((NB, BLK, BLK), BF16),
            DMA((NCHUNK,)),
        ],
        name="adjoint_blocks",
    )(sources, receptors, count, weighted, blocks)
    slots = pltpu.VMEM((GROUPS, SB, GP, BLK), BF16)
    edges = pltpu.VMEM((GROUPS, 2, STEPS, GP, LON), BF16)
    rows = pltpu.VMEM((PAD, GP, LON), F32)
    result = pl.pallas_call(
        combine_smooth,
        out_shape=jax.ShapeDtypeStruct((PROBES * LAT, LON), F32),
        in_specs=[VM, VM, VM],
        out_specs=VM,
        scratch_shapes=[pltpu.VMEM((PROBES * LAT, BLK), F32)] * 2 + [rows, rows, rows, pltpu.VMEM((GROUPS, LAT, GP, LON), F32)]
        + [slots] * 5
        + [edges] * 2
        + [DMA((GROUPS,))] * 12,
        compiler_params=remote_params(2),
        name="combine_smooth",
    )(terms.reshape(pieces), kext, flat)
    return result.reshape(PROBES, LAT, LON)


def solution(mesh):
    placed = (
        P("rcv", "src", None),
        P("src", None),
        P("src", "rcv", None, None, None),
        P("src", "rcv", None),
        P("src", "rcv", None),
        P("src", "rcv"),
        P("rcv"),
    )
    return jax.shard_map(
        per_device, mesh=mesh, in_specs=placed, out_specs=P("rcv", "src", None), check_vma=False
    )
```

time: 1020 us -> 135 us (0.13); the launches traced: 1000 us -> 133 us
  waiting for transfers between devices: 732 us -> 0 us
  Pallas kernels: 0 us -> 130 us
  other arithmetic: 125 us -> 0 us
  matrix products: 53.5 us -> 0 us
  starting transfers between devices: 40.6 us -> 0 us
  local copies, waits for them, and re-layouts: 40.5 us -> 2.26 us
  between operations: 13.5 us -> 0.69 us
    psum x1 -> x0, waiting for transfers between devices: 570 us -> none  [per_device(): receptor_all = lax.psum(sim_rows, 'src')]
    pallas_call x0 -> x5, Pallas kernels: none -> 130 us  [the longest x1 46.1 us: per_device(): pl.pallas_call(reduce_weight_gather, out_shape=jax.ShapeDtypeStruct((4, R...]
    scatter-add x12 -> x0, other arithmetic: 98.1 us -> none  [the longest x6 59.1 us: adjoint_group(): return running.at[:, source_ids].add(hessian_result * in_use[None, :, None])]
    reduce_scatter x1 -> x0, waiting for transfers between devices: 84.6 us -> none  [per_device(): lax.psum_scatter(adjoint_rows, 'rcv', scatter_dimension=0, tiled=True)]
    dot_general x12 -> x0, matrix products: 53.5 us -> none  [the longest x6 28.1 us: forward_group(): jnp.einsum('wlq,wqd->wld', block_portion, selected_entries, preferred_ele...]
    all_gather x1 -> x0, waiting for transfers between devices: 46.8 us -> none  [per_device(): gathered = lax.all_gather(local_field, 'rcv', axis=0, tiled=True)]
    ppermute x16 -> x0, starting transfers between devices: 40.4 us -> none  [the longest x8 30 us: extended(): before = lax.ppermute(last, axis, up)]
    ppermute x16 -> x0, waiting for transfers between devices: 30.1 us -> none  [the longest x8 30 us: extended(): after = lax.ppermute(leading, axis, down)]
  transfers between devices with their start and end apart: 19 -> 0, of which waited for: 11 -> 0; matrix products, arithmetic and copies ran while one was open for 0% -> 0% of each run, Pallas kernels for 0% -> 0%
where the time goes in v1:
time: 135 us; the launch traced here: 133 us
  Pallas kernels  130 us (96%)
  local copies, waits for them, and re-layouts  2.26 us (2%)
    pallas_call x1, Pallas kernels, per_device(): pl.pallas_call(reduce_weight_gather, out_shape=jax.ShapeDtypeStruct((4, R...  46.1 us
    pallas_call x1, Pallas kernels, per_device(): pl.pallas_call(combine_smooth, out_shape=jax.ShapeDtypeStruct((PROBES * L...  39.3 us
    pallas_call x1, Pallas kernels, per_device(): pl.pallas_call(smooth_gather, out_shape=(jax.ShapeDtypeStruct(pieces, BF1...  33.6 us
    pallas_call x1, Pallas kernels, per_device(): pl.pallas_call(adjoint_blocks, out_shape=jax.ShapeDtypeStruct((4, SB, PRO...  5.81 us
    pallas_call x1, Pallas kernels, per_device(): pl.pallas_call(forward_blocks, out_shape=jax.ShapeDtypeStruct((4, RB, PRO...  5.62 us

profile of v1, /device:TPU:1, one launch (start us, length us, event | category | flops | bytes accessed | tf_op | source)
XLA Modules:
  0.0 133.4 jit_solution(17909804263700374894)
XLA Ops:
  0.7 33.6 %smooth_gather.1 = (bf16[4,32,4,16,128]{4,3,2,1,0:T(8,128)(2,1)}, f32[32,256]{1,0:T(8,128)}) custom-call(bf16[1024,256]{1,0:T(8,128)(2,1)} %bitcast.15, f32[16,256]{1,0:T(8,128)} %kappa_ref.1), custom_call_target="tpu_custom_call" | custom-call | tf_op jit(solution)/shard_map/smooth_gather/pallas_call | solution.py:511
  34.3 5.6 %forward_blocks.1.part_ref = bf16[4,16,64,128]{3,2,1,0:T(8,128)(2,1)} custom-call(s32[192]{0:T(256)} %bitcast.19, s32[192]{0:T(256)} %bitcast.21, s32[1]{0:T(128)} %bitcast.9.cnt_ref, bf16[4,32,64,128]{3,2,1,0:T(8,128)(2,1)} %bitcast.17, bf16[192,128,128]{2,1,0:T(8,128)(2,1)} %bitcast.11), custom_call_target="tpu_custom_call" | custom-call | tf_op jit(solution)/shard_map/forward_blocks/pallas_call | solution.py:529
  39.9 46.1 %reduce_weight_gather.1.weighted_ref = bf16[4,16,64,128]{3,2,1,0:T(8,128)(2,1)} custom-call(bf16[4,16,64,128]{3,2,1,0:T(8,128)(2,1)} %forward_blocks.1.part_ref, f32[16,128]{1,0:T(8,128)} %bitcast.18), custom_call_target="tpu_custom_call" | custom-call | tf_op jit(solution)/shard_map/reduce_weight_gather/pallas_call | solution.py:543
  86.0 5.8 %adjoint_blocks.1 = bf16[4,32,64,128]{3,2,1,0:T(8,128)(2,1)} custom-call(s32[192]{0:T(256)} %bitcast.20, s32[192]{0:T(256)} %bitcast.22, s32[1]{0:T(128)} %bitcast.10.cnt_ref, bf16[4,16,64,128]{3,2,1,0:T(8,128)(2,1)} %reduce_weight_gather.1.weighted_ref, bf16[192,128,128]{2,1,0:T(8,128)(2,1)} %bitcast.12), custom_call_target="tpu_custom_call" | custom-call | tf_op jit(solution)/shard_map/adjoint_blocks/pallas_call | solution.py:554
  91.8 39.3 %combine_smooth.1 = f32[1024,256]{1,0:T(8,128)} custom-call(bf16[4,32,4,16,128]{4,3,2,1,0:T(8,128)(2,1)} %bitcast.13, f32[32,256]{1,0:T(8,128)} %get-tuple-element.8.kext_ref, bf16[1024,256]{1,0:T(8,128)(2,1)} %bitcast.16), custom_call_target="tpu_custom_call" | custom-call | tf_op jit(solution)/shard_map/combine_smooth/pallas_call | solution.py:569
  131.1 2.3 %copy.10 = f32[64,16,256]{2,1,0:T(8,128)} copy(f32[64,16,256]{2,1,0:T(8,128)} %bitcast.14) | data formatting | bytes 2097152
